TPU v7x, 32 devices: a whole 2x2x4 slice. The times are simulated.
32 devices in a mesh: ctx: 8 (over z, y), fsdp: 4 (over x, core).
Axes of the slice: x: 2, y: 2, z: 4, core: 2. Of those that a mesh axis runs over, the one named last changes fastest.
Arguments:
- tokens: int32 [4096], P('ctx'), may hold values from 0 to 511
- embedding: bfloat16 [512, 4096], P(None, 'fsdp'), may hold values from -6 to 6
- norm_gain: float32 [4096], replicated, may hold values from 0.1 to 1.9
- in_weight: bfloat16 [4096, 3, 2048], P('ctx', None, 'fsdp'), may hold values from -0.09375 to 0.09375
- short_taps: float32 [7, 3, 2048], P(None, None, 'fsdp'), may hold values from -2 to 2
- decay_rates: float32 [16, 128], P(None, 'fsdp'), may hold values from 0.00012207031 to 0.1
- residue: float32 [16, 128], P(None, 'fsdp'), may hold values from -0.15625 to 0.15625
- skip_weight: float32 [2048], P('fsdp'), may hold values from -4 to 4
- out_weight: bfloat16 [2048, 4096], P('fsdp', 'ctx'), may hold values from -0.125 to 0.125
Outputs:
- mixed: bfloat16 [4096, 4096], P('ctx', 'fsdp')
All inputs are finite; a program needn't handle non-finite values.
Results may differ from a plain program's by a relative error of at most 0.018.
Values may be sent and summed in bfloat16 or wider, within the bound.
No kernel may reach another device: no remote copies, remote signals or barrier semaphores. Data moves between devices by JAX's collectives and lax.ppermute only.
A program may use at most 64 MiB of HBM per device.

v0:
```python
import math
import jax
import jax.numpy as jnp
from jax import lax
from jax.sharding import PartitionSpec as P

GROUP = 16
highest_precision = lax.Precision.HIGHEST


def from_behind(value, axis, steps):
    count = lax.axis_size(axis)
    first, last = (max(0, -steps), min(count, count - steps))
    return lax.ppermute(value, axis, [(source, source + steps) for source in range(first, last)])


def direct_dft(real_part, imag_part, direction):
    length = real_part.shape[-1]
    counter = jnp.arange(length, dtype=jnp.int32)
    product = counter[:, None] * counter[None, :] % length
    angles = direction * 2.0 * math.pi / length * product.astype(jnp.float32)
    cosine_table = jnp.cos(angles)
    sine_table = jnp.sin(angles)
    new_real = jnp.dot(real_part, cosine_table, precision=highest_precision) - jnp.dot(
        imag_part, sine_table, precision=highest_precision
    )
    new_imag = jnp.dot(real_part, sine_table, precision=highest_precision) + jnp.dot(
        imag_part, cosine_table, precision=highest_precision
    )
    return (new_real, new_imag)


def transform(real_part, imag_part, direction):
    length = real_part.shape[-1]
    first_len = math.gcd(length, 128)
    if length <= 512 or first_len == 1:
        return direct_dft(real_part, imag_part, direction)
    second_len = length // first_len
    leading = real_part.shape[:-1]
    real_part = jnp.swapaxes(real_part.reshape(leading + (first_len, second_len)), -1, -2)
    imag_part = jnp.swapaxes(imag_part.reshape(leading + (first_len, second_len)), -1, -2)
    real_part, imag_part = transform(real_part, imag_part, direction)
    outer_rows = jnp.arange(second_len, dtype=jnp.int32)
    outer_cols = jnp.arange(first_len, dtype=jnp.int32)
    product = outer_rows[:, None] * outer_cols[None, :] % length
    angles = direction * 2.0 * math.pi / length * product.astype(jnp.float32)
    cosine_table = jnp.cos(angles)
    sine_table = jnp.sin(angles)
    turned_real = real_part * cosine_table - imag_part * sine_table
    turned_imag = real_part * sine_table + imag_part * cosine_table
    turned_real = jnp.swapaxes(turned_real, -1, -2)
    turned_imag = jnp.swapaxes(turned_imag, -1, -2)
    turned_real, turned_imag = transform(turned_real, turned_imag, direction)
    turned_real = jnp.swapaxes(turned_real, -1, -2).reshape(leading + (length,))
    turned_imag = jnp.swapaxes(turned_imag, -1, -2).reshape(leading + (length,))
    return (turned_real, turned_imag)


def modal_spectrum(decay_rates, residue, frequency, seq_length):
    rate_grid = decay_rates[:, :, None]
    angle_grid = math.pi / seq_length * frequency
    parity = frequency - 2.0 * jnp.floor(0.5 * frequency)
    tail_term = -jnp.expm1(-rate_grid * seq_length)
    numerator = residue[:, :, None] * (tail_term + parity * (2.0 - 2.0 * tail_term))
    half_sine = jnp.sin(0.5 * angle_grid)
    real_den = 2.0 * half_sine * half_sine + -jnp.expm1(-rate_grid) * jnp.cos(angle_grid)
    imag_den = jnp.exp(-rate_grid) * jnp.sin(angle_grid)
    magnitude = real_den * real_den + imag_den * imag_den
    spec_real = jnp.sum(numerator * real_den / magnitude, axis=0)
    spec_imag = jnp.sum(-numerator * imag_den / magnitude, axis=0)
    return (spec_real, spec_imag)


def by_transpose(pair_real, pair_imag, decay_rates, residue, position):
    tok_count = pair_real.shape[-1]
    ctx_count = lax.axis_size("ctx")
    seq_length = tok_count * ctx_count
    pair_half = GROUP // 2
    moved_real, moved_imag = (
        lax.all_to_all(
            pair_real.astype(jnp.bfloat16), "ctx", split_axis=0, concat_axis=1, tiled=True
        ).astype(pair_real.dtype),
        lax.all_to_all(
            pair_imag.astype(jnp.bfloat16), "ctx", split_axis=0, concat_axis=1, tiled=True
        ).astype(pair_imag.dtype),
    )
    pair_count = moved_real.shape[0]
    padded_real = jnp.concatenate([moved_real, jnp.zeros_like(moved_real)], axis=1)
    padded_imag = jnp.concatenate([moved_imag, jnp.zeros_like(moved_imag)], axis=1)
    spec_in_real, spec_in_imag = transform(padded_real, padded_imag, -1.0)
    pair_decay = lax.dynamic_slice_in_dim(
        jnp.repeat(decay_rates, pair_half, axis=1), position * pair_count, pair_count, 1
    )
    pair_residue = lax.dynamic_slice_in_dim(
        jnp.repeat(residue, pair_half, axis=1), position * pair_count, pair_count, 1
    )
    frequency = jnp.arange(2 * seq_length, dtype=jnp.int32).astype(jnp.float32)
    spec_real, spec_imag = modal_spectrum(pair_decay, pair_residue, frequency, seq_length)
    prod_real = spec_in_real * spec_real - spec_in_imag * spec_imag
    prod_imag = spec_in_real * spec_imag + spec_in_imag * spec_real
    back_real, back_imag = transform(prod_real, prod_imag, 1.0)
    back_real = back_real[:, :seq_length] / (2 * seq_length)
    back_imag = back_imag[:, :seq_length] / (2 * seq_length)
    return (
        lax.all_to_all(
            back_real.astype(jnp.bfloat16), "ctx", split_axis=1, concat_axis=0, tiled=True
        ).astype(back_real.dtype),
        lax.all_to_all(
            back_imag.astype(jnp.bfloat16), "ctx", split_axis=1, concat_axis=0, tiled=True
        ).astype(back_imag.dtype),
    )


def body(
    tokens,
    embedding,
    norm_gain,
    in_weight,
    short_taps,
    decay_rates,
    residue,
    skip_weight,
    out_weight,
):
    tok_count = tokens.shape[0]
    vocab_size = embedding.shape[0]
    local_channels = in_weight.shape[2]
    one_hot = (tokens[:, None] == jnp.arange(vocab_size, dtype=jnp.int32)[None, :]).astype(
        jnp.bfloat16
    )
    own_columns = jnp.dot(one_hot, embedding, preferred_element_type=jnp.float32).astype(
        jnp.bfloat16
    )
    features = lax.all_gather(own_columns, "fsdp", axis=1, tiled=True)
    widened = features.astype(jnp.float32)
    mean_square = jnp.mean(widened * widened, axis=1, keepdims=True)
    normed = (widened * lax.rsqrt(mean_square + 1e-05) * norm_gain).astype(jnp.bfloat16)
    block_piece = lax.all_gather(in_weight, "ctx", axis=0, tiled=True)
    panel = block_piece.reshape(block_piece.shape[0], 3 * local_channels)
    projected = jnp.dot(normed, panel, preferred_element_type=jnp.float32)
    projected = projected.reshape(tok_count, 3, local_channels).astype(jnp.bfloat16)
    reach_back = short_taps.shape[0] - 1
    earlier = from_behind(projected[tok_count - reach_back :], "ctx", 1)
    extended = jnp.concatenate([earlier, projected], axis=0).astype(jnp.float32)
    short = jnp.zeros((tok_count, 3, local_channels), jnp.float32)
    for lag_step in range(reach_back + 1):
        short = (
            short
            + short_taps[lag_step]
            * extended[reach_back - lag_step : reach_back - lag_step + tok_count]
        )
    queries = short[:, 0, :]
    driving = short[:, 1, :] * short[:, 2, :]
    groups_local = local_channels // GROUP
    pair_half = GROUP // 2
    flipped = driving.T.reshape(groups_local, 2, pair_half, tok_count)
    pair_real = flipped[:, 0].reshape(groups_local * pair_half, tok_count)
    pair_imag = flipped[:, 1].reshape(groups_local * pair_half, tok_count)
    position = lax.axis_index("ctx")
    conv_real, conv_imag = by_transpose(pair_real, pair_imag, decay_rates, residue, position)
    stacked = jnp.stack(
        [
            conv_real.reshape(groups_local, pair_half, tok_count),
            conv_imag.reshape(groups_local, pair_half, tok_count),
        ],
        axis=1,
    )
    convolved = stacked.reshape(local_channels, tok_count).T
    response = convolved + skip_weight * driving
    gated = (queries * response).astype(jnp.bfloat16)
    partial_out = jnp.dot(
        gated,
        lax.all_gather(out_weight, "ctx", axis=1, tiled=True),
        preferred_element_type=jnp.float32,
    )
    return lax.psum_scatter(
        partial_out.astype(jnp.bfloat16), "fsdp", scatter_dimension=1, tiled=True
    )


def solution(mesh):
    placed = (
        P("ctx"),
        P(None, "fsdp"),
        P(),
        P("ctx", None, "fsdp"),
        P(None, None, "fsdp"),
        P(None, "fsdp"),
        P(None, "fsdp"),
        P("fsdp"),
        P("fsdp", "ctx"),
    )
    return jax.shard_map(
        body, mesh=mesh, in_specs=placed, out_specs=P("ctx", "fsdp"), check_vma=False
    )
```

profile of v0, /device:TPU:0, one launch (start us, length us, event | category | flops | bytes accessed | tf_op | source)
XLA Modules:
  0.0 412.2 jit_solution(13552553999425592223)
XLA Ops:
  7.8 2.4 convolution_convert_fusion.1
  10.3 1.6 copy.98
  13.2 34.4 %all-gather.4.cloned.1.call-done = bf16[512,4096]{1,0:T(8,128)(2,1)} async-done(((bf16[512,1024]{1,0:T(8,128)(2,1)}), bf16[512,4096]{1,0:T(8,128)(2,1)}) %all-gather.4.cloned.1.call-update) | async-done | bytes 4194320 | tf_op jit(solution)/shard_map/all_gather | solution.py:134
  47.5 3.1 fusion.6
  50.6 175.1 %all-gather.6.cloned.1.call-done = bf16[4096,3,512]{0,2,1:T(8,128)(2,1)} async-done(((bf16[512,3,512]{0,2,1:T(8,128)(2,1)}), bf16[4096,3,512]{0,2,1:T(8,128)(2,1)}) %all-gather.6.cloned.1.call-update) | async-done | bytes 12582928 | tf_op jit(solution)/shard_map/all_gather | solution.py:138
  225.7 11.0 %fusion.27 = bf16[512,3,512]{2,0,1:T(8,128)(2,1)S(1)} fusion(bf16[4096,3,512]{0,2,1:T(8,128)(2,1)} %all-gather.6.cloned.1.call-done, bf16[512,4096]{1,0:T(8,128)(2,1)} %all-gather.4.cloned.1.call-done, f32[4096]{0:T(1024)S(1)} %copy-done.8, f32[512]{0:T(512)S(1)} %add_rsqrt_fusion), kind=kOutput, calls=%fused_computation.43 | convolution fusion | flops 6451625984 | bytes 18368512 | tf_op jit(solution)/shard_map/dot_general | solution.py:140
  236.8 3.4 collective-permute-start
  242.1 2.6 fusion.13
  244.7 1.7 copy-done.2
  247.6 6.3 %all-to-all-start = ((bf16[8,32,512]{2,1,0:T(8,128)(2,1)}), bf16[8,32,512]{2,1,0:T(8,128)(2,1)S(1)}, u32[]{:S(2)}, u32[]{:S(2)}) async-start(bf16[8,32,512]{2,1,0:T(8,128)(2,1)} %bitcast.8), calls=%async_computation | async-start | bytes 524288 | tf_op jit(solution)/shard_map/all_to_all | solution.py:80
  253.9 10.2 %fusion.3 = (f32[32,8192]{1,0:T(8,128)S(1)}, f32[32,8192]{1,0:T(8,128)S(1)}) fusion(f32[8192]{0:T(1024)S(1)} %get-tuple-element.34, f32[16,32]{1,0:T(8,128)S(1)} %get-tuple-element.21, f32[8192]{0:T(1024)S(1)} %get-tuple-element.35, f32[16,32]{1,0:T(8,128)S(1)} %get-tuple-element.20, f32[8192]{0:T(1024)S(1)} %get-tuple-element.32, ...), kind=kLoop, calls=%fused_computation.8 | loop fusion | flops 66584576 | bytes 2238464 | tf_op jit(solution)/shard_map/reduce_sum | solution.py:70
  264.1 2.1 reduce_sum.33
  266.2 2.2 reduce_sum.35
  268.4 6.0 %all-to-all-start.1 = ((bf16[8,32,512]{2,1,0:T(8,128)(2,1)}), bf16[8,32,512]{2,1,0:T(8,128)(2,1)S(1)}, u32[]{:S(2)}, u32[]{:S(2)}) async-start(bf16[8,32,512]{2,1,0:T(8,128)(2,1)} %bitcast.12), calls=%async_computation.1 | async-start | bytes 524288 | tf_op jit(solution)/shard_map/all_to_all | solution.py:83
  276.3 1.8 fusion.56
  278.1 13.8 %all-to-all-done.1 = bf16[8,32,512]{2,1,0:T(8,128)(2,1)S(1)} async-done(((bf16[8,32,512]{2,1,0:T(8,128)(2,1)}), bf16[8,32,512]{2,1,0:T(8,128)(2,1)S(1)}, u32[]{:S(2)}, u32[]{:S(2)}) %all-to-all-start.1) | async-done | bytes 262176 | tf_op jit(solution)/shard_map/all_to_all | solution.py:83
  293.5 2.1 fusion.47
  298.6 1.3 fusion.45
  299.9 1.7 reshape.200
  302.9 2.3 fusion.44
  305.2 3.3 reshape.203
  308.5 3.7 multiply_subtract_fusion
  312.2 3.5 fusion.21
  315.7 3.5 fusion.19
  319.3 3.5 fusion.35
  322.8 3.7 fusion.41
  326.5 1.3 fusion.66
  330.5 3.6 all-to-all-start.2
  337.5 4.9 %all-to-all-done.2 = bf16[32,8,512]{2,0,1:T(8,128)(2,1)S(1)} async-done(((bf16[32,8,512]{2,0,1:T(8,128)(2,1)}), bf16[32,8,512]{2,0,1:T(8,128)(2,1)S(1)}, u32[]{:S(2)}, u32[]{:S(2)}) %all-to-all-start.2) | async-done | bytes 262176 | tf_op jit(solution)/shard_map/all_to_all | solution.py:105
  342.3 11.6 %all_to_all.46 = bf16[32,8,512]{2,0,1:T(8,128)(2,1)S(1)} all-to-all(bf16[32,8,512]{2,0,1:T(8,128)(2,1)S(1)} %bitcast.180), channel_id=1, replica_groups=mesh['ctx'=8,'fsdp'=4] {'ctx'}, dimensions={1} | all-to-all | bytes 524288 | tf_op jit(solution)/shard_map/all_to_all | solution.py:108
  354.5 7.6 %convolution_convert_fusion = bf16[512,4096]{1,0:T(8,128)(2,1)} fusion(bf16[512,4096]{1,0:T(8,128)(2,1)} %all-gather.8.cloned.1.call-done, f32[512,3,512]{2,0,1:T(8,128)} %copy-done.2, f32[512,512]{0,1:T(8,128)S(1)} %copy.115, f32[512]{0:T(512)S(1)} %copy-done.9), kind=kOutput, calls=%fused_computation.16 | convolution fusion | flops 2150891520 | bytes 12584960 | tf_op jit(solution)/shard_map/dot_general | solution.py:171
  362.1 43.4 %reduce-scatter.2.cloned.1.call-done = bf16[512,1024]{1,0:T(8,128)(2,1)} async-done(((bf16[512,4096]{1,0:T(8,128)(2,1)}), bf16[512,1024]{1,0:T(8,128)(2,1)}) %reduce-scatter.2.cloned.1.call-update) | async-done | bytes 1048592 | tf_op jit(solution)/shard_map/reduce_scatter | solution.py:176
  (77 shorter events, 19.9 us)
Async XLA Ops:
  6.5 1.2 copy-start
  6.5 3.7 copy-start.4
  6.5 41.0 %all-gather.4.cloned.1.call-start = ((), (), s32[]{:S(2)}) async-start(), calls=%async_computation.5 | async-start | bytes 5242880 | tf_op jit(solution)/shard_map/all_gather | solution.py:134
  10.2 2.6 copy-start.5
  10.2 2.6 copy-start.6
  10.2 2.7 copy-start.7
  10.2 215.5 %all-gather.6.cloned.1.call-start = ((), (), s32[]{:S(2)}) async-start(), calls=%async_computation.6 | async-start | bytes 14155776 | tf_op jit(solution)/shard_map/all_gather | solution.py:138
  11.9 213.9 %copy-start.8 = (f32[4096]{0:T(1024)S(1)}, f32[4096]{0:T(1024)}, u32[]{:S(2)}) copy-start(f32[4096]{0:T(1024)} %param.11) | copy-start | bytes 49156
  11.9 342.6 %all-gather.8.cloned.1.call-start = ((), (), s32[]{:S(2)}) async-start(), calls=%async_computation.7 | async-start | bytes 4718592 | tf_op jit(solution)/shard_map/all_gather | solution.py:173
  236.8 4.9 %collective-permute-start = (bf16[6,3,512]{2,0,1:T(8,128)(2,1)S(1)}, bf16[6,3,512]{2,0,1:T(8,128)(2,1)S(1)}, u32[]{:S(2)}, u32[]{:S(2)}) collective-permute-start(bf16[6,3,512]{2,0,1:T(8,128)(2,1)S(1)} %slice.90), channel_id=1, source_target_pairs={{0,4},{4,8},{8,12},{12,16},{16,20},{20,24},{24,28},{1,5},{5,9},{9,... | collective-permute-start | bytes 55304 | tf_op jit(solution)/shard_map/ppermute | solution.py:14
  244.7 1.7 copy-start.2
  247.6 20.8 %all-to-all-start = ((bf16[8,32,512]{2,1,0:T(8,128)(2,1)}), bf16[8,32,512]{2,1,0:T(8,128)(2,1)S(1)}, u32[]{:S(2)}, u32[]{:S(2)}) async-start(bf16[8,32,512]{2,1,0:T(8,128)(2,1)} %bitcast.8), calls=%async_computation | async-start | bytes 524288 | tf_op jit(solution)/shard_map/all_to_all | solution.py:80
  268.4 23.5 %all-to-all-start.1 = ((bf16[8,32,512]{2,1,0:T(8,128)(2,1)}), bf16[8,32,512]{2,1,0:T(8,128)(2,1)S(1)}, u32[]{:S(2)}, u32[]{:S(2)}) async-start(bf16[8,32,512]{2,1,0:T(8,128)(2,1)} %bitcast.12), calls=%async_computation.1 | async-start | bytes 524288 | tf_op jit(solution)/shard_map/all_to_all | solution.py:83
  305.2 3.3 copy-start.3
  330.5 11.8 %all-to-all-start.2 = ((bf16[32,8,512]{2,0,1:T(8,128)(2,1)}), bf16[32,8,512]{2,0,1:T(8,128)(2,1)S(1)}, u32[]{:S(2)}, u32[]{:S(2)}) async-start(bf16[32,8,512]{2,0,1:T(8,128)(2,1)} %bitcast.168), calls=%async_computation.2 | async-start | bytes 524288 | tf_op jit(solution)/shard_map/all_to_all | solution.py:105
  334.1 71.4 %reduce-scatter.2.cloned.1.call-start = ((), (), s32[]{:S(2)}) async-start(), calls=%async_computation.8 | async-start | bytes 5242880 | tf_op jit(solution)/shard_map/reduce_scatter | solution.py:176
  342.3 12.1 %copy-start.9 = (f32[512]{0:T(512)S(1)}, f32[512]{0:T(512)}, u32[]{:S(2)}) copy-start(f32[512]{0:T(512)} %param.16) | copy-start | bytes 6148
  354.5 51.0 %copy-start.1 = (bf16[512,1024]{1,0:T(8,128)(2,1)S(1)}, bf16[512,1024]{1,0:T(8,128)(2,1)}, u32[]{:S(2)}) copy-start(bf16[512,1024]{1,0:T(8,128)(2,1)} %param.10) | copy-start | bytes 3145732
Sparse Core Ops, SparseCore 0:
  10.3 37.1 all-gather.3
  49.6 176.1 all-gather.5
  227.8 81.8 all-gather.7
  362.2 43.2 reduce-scatter.1
where the time goes:
time: 418 us; the launch traced here: 412 us
  waiting for transfers between devices  274 us (66%)
  matrix products  52.2 us (12%)
  other arithmetic  20.9 us (5%)
  local copies, waits for them, and re-layouts  20.7 us (5%)
  starting transfers between devices  19.4 us (5%)
  between operations  13.8 us (3%)
  blocking collectives  11.6 us (3%)
    all_gather x1, waiting for transfers between devices, body(): block_piece = lax.all_gather(in_weight, 'ctx', axis=0, tiled=True)  175 us
    reduce_scatter x1, waiting for transfers between devices, body(): lax.psum_scatter(partial_out.astype(jnp.bfloat16), 'fsdp', scatter_dimens...  43.4 us
    all_gather x1, waiting for transfers between devices, body(): features = lax.all_gather(own_columns, 'fsdp', axis=1, tiled=True)  34.4 us
    all_to_all x1, waiting for transfers between devices, by_transpose(): lax.all_to_all(pair_imag.astype(jnp.bfloat16), 'ctx', split_axis=0, conca...  13.8 us
    all_to_all x1, blocking collectives, by_transpose(): lax.all_to_all(back_imag.astype(jnp.bfloat16), 'ctx', split_axis=1, conca...  11.6 us
    dot_general x1, matrix products, body(): projected = jnp.dot(normed, panel, preferred_element_type=jnp.float32)  11 us
    reduce_sum x1, other arithmetic, modal_spectrum(): spec_imag = jnp.sum(-numerator * imag_den / magnitude, axis=0)  10.2 us
  transfers between devices with their start and end apart: 8, of which 6 were waited for; matrix products, arithmetic and copies ran while one was open for 20% of the time, Pallas kernels for 0%

commit v1 on v0

--- a/solution.py
+++ b/solution.py
@@ -131,7 +131,16 @@
     own_columns = jnp.dot(one_hot, embedding, preferred_element_type=jnp.float32).astype(
         jnp.bfloat16
     )
-    features = lax.all_gather(own_columns, "fsdp", axis=1, tiled=True)
+    ways = lax.axis_size("fsdp")
+    up = [(d, (d + 1) % ways) for d in range(ways)]
+    down = [(d, (d - 1) % ways) for d in range(ways)]
+    earlier_2, later = ([own_columns], [own_columns])
+    for _ in range(ways // 2):
+        earlier_2.append(lax.ppermute(earlier_2[-1], "fsdp", up))
+    for _ in range((ways - 1) // 2):
+        later.append(lax.ppermute(later[-1], "fsdp", down))
+    line = jnp.concatenate([*earlier_2[::-1], *later[1:]], axis=1)
+    features = jnp.roll(line, (lax.axis_index("fsdp") - ways // 2) * own_columns.shape[1], axis=1)
     widened = features.astype(jnp.float32)
     mean_square = jnp.mean(widened * widened, axis=1, keepdims=True)
     normed = (widened * lax.rsqrt(mean_square + 1e-05) * norm_gain).astype(jnp.bfloat16)

time: 418 us -> 381 us (0.911)
  waiting for transfers between devices: 274 us -> 229 us
  local copies, waits for them, and re-layouts: 20.7 us -> 26.9 us
  starting transfers between devices: 19.4 us -> 24.4 us
    all_gather x1, waiting for transfers between devices: 175 us -> 133 us  [body(): block_piece = lax.all_gather(in_weight, 'ctx', axis=0, tiled=True)]
    all_gather x1 -> x0, waiting for transfers between devices: 34.4 us -> none  [body(): features = lax.all_gather(own_columns, 'fsdp', axis=1, tiled=True)]
    ppermute x0 -> x3, waiting for transfers between devices: none -> 32.4 us  [the longest x2 32.4 us: body(): earlier_2.append(lax.ppermute(earlier_2[-1], 'fsdp', up))]
    unnamed x30 -> x39, local copies, waits for them, and re-layouts: 5.97 us -> 12.1 us
    ppermute x0 -> x3, starting transfers between devices: none -> 4.97 us  [the longest x2 2.99 us: body(): earlier_2.append(lax.ppermute(earlier_2[-1], 'fsdp', up))]
  transfers between devices with their start and end apart: 8 -> 10, of which waited for: 6 -> 7; matrix products, arithmetic and copies ran while one was open for 20% -> 22% of each run, Pallas kernels for 0% -> 0%
where the time goes in v1:
time: 381 us; the launch traced here: 375 us
  waiting for transfers between devices  229 us (60%)
  matrix products  50.6 us (13%)
  local copies, waits for them, and re-layouts  26.9 us (7%)
  starting transfers between devices  24.4 us (6%)
  other arithmetic  18.7 us (5%)
  between operations  13.9 us (4%)
  blocking collectives  11.4 us (3%)
    all_gather x1, waiting for transfers between devices, body(): block_piece = lax.all_gather(in_weight, 'ctx', axis=0, tiled=True)  133 us
    reduce_scatter x1, waiting for transfers between devices, body(): lax.psum_scatter(partial_out.astype(jnp.bfloat16), 'fsdp', scatter_dimens...  43.4 us
    ppermute x2, waiting for transfers between devices, body(): earlier_2.append(lax.ppermute(earlier_2[-1], 'fsdp', up))  32.4 us
    all_to_all x1, waiting for transfers between devices, by_transpose(): lax.all_to_all(pair_imag.astype(jnp.bfloat16), 'ctx', split_axis=0, conca...  13.8 us
    unnamed x39, local copies, waits for them, and re-layouts  12.1 us
    all_to_all x1, blocking collectives, by_transpose(): lax.all_to_all(back_imag.astype(jnp.bfloat16), 'ctx', split_axis=1, conca...  11.4 us
    dot_general x1, matrix products, body(): projected = jnp.dot(normed, panel, preferred_element_type=jnp.float32)  11 us
    reduce_sum x1, other arithmetic, modal_spectrum(): spec_imag = jnp.sum(-numerator * imag_den / magnitude, axis=0)  10.2 us
  transfers between devices with their start and end apart: 10, of which 7 were waited for; matrix products, arithmetic and copies ran while one was open for 22% of the time, Pallas kernels for 0%

profile of v1, /device:TPU:0, one launch (start us, length us, event | category | flops | bytes accessed | tf_op | source)
XLA Modules:
  0.0 374.6 jit_solution(11674129652551626426)
XLA Ops:
  6.5 2.7 copy.98
  10.6 2.0 collective-permute-start.2
  12.9 20.8 %collective-permute-done = bf16[512,1024]{1,0:T(8,128)(2,1)S(1)} collective-permute-done((bf16[512,1024]{1,0:T(8,128)(2,1)S(1)}, bf16[512,1024]{1,0:T(8,128)(2,1)S(1)}, u32[]{:S(2)}, u32[]{:S(2)}) %collective-permute-start) | collective-permute-done | bytes 1048608 | tf_op jit(solution)/shard_map/ppermute | solution.py:139
  33.7 2.4 collective-permute-start.1
  36.4 11.6 %collective-permute-done.1 = bf16[512,1024]{1,0:T(8,128)(2,1)} collective-permute-done((bf16[512,1024]{1,0:T(8,128)(2,1)S(1)}, bf16[512,1024]{1,0:T(8,128)(2,1)}, u32[]{:S(2)}, u32[]{:S(2)}) %collective-permute-start.1) | collective-permute-done | bytes 1048608 | tf_op jit(solution)/shard_map/ppermute | solution.py:139
  51.3 3.2 copy-done.4
  55.4 132.9 %all-gather.3.cloned.1.call-done = bf16[4096,3,512]{0,2,1:T(8,128)(2,1)} async-done(((bf16[512,3,512]{0,2,1:T(8,128)(2,1)}), bf16[4096,3,512]{0,2,1:T(8,128)(2,1)}) %all-gather.3.cloned.1.call-update) | async-done | bytes 12582928 | tf_op jit(solution)/shard_map/all_gather | solution.py:147
  188.3 11.0 %fusion.28 = bf16[512,3,512]{2,0,1:T(8,128)(2,1)S(1)} fusion(bf16[4096,3,512]{0,2,1:T(8,128)(2,1)} %all-gather.3.cloned.1.call-done, f32[4096]{0:T(1024)S(1)} %copy-done.8, f32[512]{0:T(512)S(1)} %add_rsqrt_fusion, bf16[512,8192]{1,0:T(8,128)(2,1)} %copy-done.4, s32[]{:T(128)S(6)} %select_n.101), kind=kOutput, calls=%fused_computation.44 | convolution fusion | flops 6451625984 | bytes 18368516 | tf_op jit(solution)/shard_map/dot_general | solution.py:149
  199.3 3.4 collective-permute-start.3
  204.6 2.6 fusion.14
  207.3 1.7 copy-done.2
  210.1 6.3 %all-to-all-start = ((bf16[8,32,512]{2,1,0:T(8,128)(2,1)}), bf16[8,32,512]{2,1,0:T(8,128)(2,1)S(1)}, u32[]{:S(2)}, u32[]{:S(2)}) async-start(bf16[8,32,512]{2,1,0:T(8,128)(2,1)} %bitcast.8), calls=%async_computation | async-start | bytes 524288 | tf_op jit(solution)/shard_map/all_to_all | solution.py:80
  216.4 10.2 %fusion.3 = (f32[32,8192]{1,0:T(8,128)S(1)}, f32[32,8192]{1,0:T(8,128)S(1)}) fusion(f32[8192]{0:T(1024)S(1)} %get-tuple-element.34, f32[16,32]{1,0:T(8,128)S(1)} %get-tuple-element.21, f32[8192]{0:T(1024)S(1)} %get-tuple-element.35, f32[16,32]{1,0:T(8,128)S(1)} %get-tuple-element.20, f32[8192]{0:T(1024)S(1)} %get-tuple-element.32, ...), kind=kLoop, calls=%fused_computation.8 | loop fusion | flops 66584576 | bytes 2238464 | tf_op jit(solution)/shard_map/reduce_sum | solution.py:70
  226.6 2.1 reduce_sum.33
  228.7 2.2 reduce_sum.35
  230.9 6.0 %all-to-all-start.1 = ((bf16[8,32,512]{2,1,0:T(8,128)(2,1)}), bf16[8,32,512]{2,1,0:T(8,128)(2,1)S(1)}, u32[]{:S(2)}, u32[]{:S(2)}) async-start(bf16[8,32,512]{2,1,0:T(8,128)(2,1)} %bitcast.12), calls=%async_computation.1 | async-start | bytes 524288 | tf_op jit(solution)/shard_map/all_to_all | solution.py:83
  238.8 1.8 fusion.57
  240.6 13.8 %all-to-all-done.1 = bf16[8,32,512]{2,1,0:T(8,128)(2,1)S(1)} async-done(((bf16[8,32,512]{2,1,0:T(8,128)(2,1)}), bf16[8,32,512]{2,1,0:T(8,128)(2,1)S(1)}, u32[]{:S(2)}, u32[]{:S(2)}) %all-to-all-start.1) | async-done | bytes 262176 | tf_op jit(solution)/shard_map/all_to_all | solution.py:83
  256.1 2.1 fusion.48
  262.4 1.7 reshape.200
  265.4 2.3 fusion.45
  267.7 3.3 reshape.203
  271.0 3.7 multiply_subtract_fusion
  274.7 3.5 fusion.22
  278.2 3.5 fusion.20
  281.8 3.5 fusion.36
  285.3 3.7 fusion.42
  293.0 3.7 all-to-all-start.2
  300.0 4.8 %all-to-all-done.2 = bf16[32,8,512]{2,0,1:T(8,128)(2,1)S(1)} async-done(((bf16[32,8,512]{2,0,1:T(8,128)(2,1)}), bf16[32,8,512]{2,0,1:T(8,128)(2,1)S(1)}, u32[]{:S(2)}, u32[]{:S(2)}) %all-to-all-start.2) | async-done | bytes 262176 | tf_op jit(solution)/shard_map/all_to_all | solution.py:105
  304.9 11.4 %all_to_all.46 = bf16[32,8,512]{2,0,1:T(8,128)(2,1)S(1)} all-to-all(bf16[32,8,512]{2,0,1:T(8,128)(2,1)S(1)} %bitcast.180), channel_id=1, replica_groups=mesh['ctx'=8,'fsdp'=4] {'ctx'}, dimensions={1} | all-to-all | bytes 524288 | tf_op jit(solution)/shard_map/all_to_all | solution.py:108
  316.8 7.6 %convolution_convert_fusion = bf16[512,4096]{1,0:T(8,128)(2,1)} fusion(bf16[512,4096]{1,0:T(8,128)(2,1)} %all-gather.5.cloned.1.call-done, f32[512,3,512]{2,0,1:T(8,128)} %copy-done.2, f32[512,512]{0,1:T(8,128)S(1)} %copy.115, f32[512]{0:T(512)S(1)} %copy-done.10), kind=kOutput, calls=%fused_computation.16 | convolution fusion | flops 2150891520 | bytes 12584960 | tf_op jit(solution)/shard_map/dot_general | solution.py:180
  324.4 43.4 %reduce-scatter.2.cloned.1.call-done = bf16[512,1024]{1,0:T(8,128)(2,1)} async-done(((bf16[512,4096]{1,0:T(8,128)(2,1)}), bf16[512,1024]{1,0:T(8,128)(2,1)}) %reduce-scatter.2.cloned.1.call-update) | async-done | bytes 1048592 | tf_op jit(solution)/shard_map/reduce_scatter | solution.py:185
  (90 shorter events, 26.0 us)
Async XLA Ops:
  6.5 2.8 copy-start
  6.5 2.8 copy-start.9
  6.5 181.7 %all-gather.3.cloned.1.call-start = ((), (), s32[]{:S(2)}) async-start(), calls=%async_computation.5 | async-start | bytes 14155776 | tf_op jit(solution)/shard_map/all_gather | solution.py:147
  9.2 3.4 copy-start.6
  9.2 3.5 copy-start.7
  9.2 3.6 copy-start.5
  9.3 307.5 %all-gather.5.cloned.1.call-start = ((), (), s32[]{:S(2)}) async-start(), calls=%async_computation.6 | async-start | bytes 4718592 | tf_op jit(solution)/shard_map/all_gather | solution.py:182
  10.1 23.6 %collective-permute-start = (bf16[512,1024]{1,0:T(8,128)(2,1)S(1)}, bf16[512,1024]{1,0:T(8,128)(2,1)S(1)}, u32[]{:S(2)}, u32[]{:S(2)}) collective-permute-start(bf16[512,1024]{1,0:T(8,128)(2,1)S(1)} %convolution_convert_fusion.1), channel_id=1, source_target_pairs={{0,1},{1,2},{2,3},{3,0},{4,5},{5,6},{6,7},{7,4},{8,9},{9,10},{10,1... | collective-permute-start | bytes 3145736 | tf_op jit(solution)/shard_map/ppermute | solution.py:139
  10.6 38.9 %collective-permute-start.2 = (bf16[512,1024]{1,0:T(8,128)(2,1)S(1)}, bf16[512,1024]{1,0:T(8,128)(2,1)S(1)}, u32[]{:S(2)}, u32[]{:S(2)}) collective-permute-start(bf16[512,1024]{1,0:T(8,128)(2,1)S(1)} %convolution_convert_fusion.1), channel_id=1, source_target_pairs={{0,3},{1,0},{2,1},{3,2},{4,7},{5,4},{6,5},{7,6},{8,11},{9,8},{10,9... | collective-permute-start | bytes 3145736 | tf_op jit(solution)/shard_map/ppermute | solution.py:141
  33.7 14.3 %collective-permute-start.1 = (bf16[512,1024]{1,0:T(8,128)(2,1)S(1)}, bf16[512,1024]{1,0:T(8,128)(2,1)}, u32[]{:S(2)}, u32[]{:S(2)}) collective-permute-start(bf16[512,1024]{1,0:T(8,128)(2,1)S(1)} %collective-permute-done), channel_id=1, source_target_pairs={{0,1},{1,2},{2,3},{3,0},{4,5},{5,6},{6,7},{7,4},{8,9},{9,10},{10,1... | collective-permute-start | bytes 3145736 | tf_op jit(solution)/shard_map/ppermute | solution.py:139
  51.1 137.1 %copy-start.8 = (f32[4096]{0:T(1024)S(1)}, f32[4096]{0:T(1024)}, u32[]{:S(2)}) copy-start(f32[4096]{0:T(1024)} %param.11) | copy-start | bytes 49156
  51.2 3.2 copy-start.4
  199.3 4.9 %collective-permute-start.3 = (bf16[6,3,512]{2,0,1:T(8,128)(2,1)S(1)}, bf16[6,3,512]{2,0,1:T(8,128)(2,1)S(1)}, u32[]{:S(2)}, u32[]{:S(2)}) collective-permute-start(bf16[6,3,512]{2,0,1:T(8,128)(2,1)S(1)} %slice.90), channel_id=1, source_target_pairs={{0,4},{4,8},{8,12},{12,16},{16,20},{20,24},{24,28},{1,5},{5,9},{9,... | collective-permute-start | bytes 55304 | tf_op jit(solution)/shard_map/ppermute | solution.py:14
  207.2 1.7 copy-start.2
  210.1 20.8 %all-to-all-start = ((bf16[8,32,512]{2,1,0:T(8,128)(2,1)}), bf16[8,32,512]{2,1,0:T(8,128)(2,1)S(1)}, u32[]{:S(2)}, u32[]{:S(2)}) async-start(bf16[8,32,512]{2,1,0:T(8,128)(2,1)} %bitcast.8), calls=%async_computation | async-start | bytes 524288 | tf_op jit(solution)/shard_map/all_to_all | solution.py:80
  230.9 23.5 %all-to-all-start.1 = ((bf16[8,32,512]{2,1,0:T(8,128)(2,1)}), bf16[8,32,512]{2,1,0:T(8,128)(2,1)S(1)}, u32[]{:S(2)}, u32[]{:S(2)}) async-start(bf16[8,32,512]{2,1,0:T(8,128)(2,1)} %bitcast.12), calls=%async_computation.1 | async-start | bytes 524288 | tf_op jit(solution)/shard_map/all_to_all | solution.py:83
  267.7 3.3 copy-start.3
  293.0 11.9 %all-to-all-start.2 = ((bf16[32,8,512]{2,0,1:T(8,128)(2,1)}), bf16[32,8,512]{2,0,1:T(8,128)(2,1)S(1)}, u32[]{:S(2)}, u32[]{:S(2)}) async-start(bf16[32,8,512]{2,0,1:T(8,128)(2,1)} %bitcast.168), calls=%async_computation.2 | async-start | bytes 524288 | tf_op jit(solution)/shard_map/all_to_all | solution.py:105
  296.6 71.2 %reduce-scatter.2.cloned.1.call-start = ((), (), s32[]{:S(2)}) async-start(), calls=%async_computation.7 | async-start | bytes 5242880 | tf_op jit(solution)/shard_map/reduce_scatter | solution.py:185
  300.0 16.8 %copy-start.10 = (f32[512]{0:T(512)S(1)}, f32[512]{0:T(512)}, u32[]{:S(2)}) copy-start(f32[512]{0:T(512)} %param.16) | copy-start | bytes 6148
  316.8 51.1 %copy-start.1 = (bf16[512,1024]{1,0:T(8,128)(2,1)S(1)}, bf16[512,1024]{1,0:T(8,128)(2,1)}, u32[]{:S(2)}) copy-start(bf16[512,1024]{1,0:T(8,128)(2,1)} %param.10) | copy-start | bytes 3145732
Sparse Core Ops, SparseCore 0:
  9.4 178.8 all-gather.2
  190.3 81.9 all-gather.4
  324.6 43.2 reduce-scatter.1
